TPU v7x, 512 devices: a whole 4x4x16 slice. The times are simulated.
512 devices in a mesh: section: 16 (over y, x), rows: 32 (over z, core).
Axes of the slice: x: 4, y: 4, z: 16, core: 2. Of those that a mesh axis runs over, the one named last changes fastest.
Arguments:
- activations: bfloat16 [128, 64, 64, 128], P('section', 'rows'), may hold values from -48 to 48
- first_cache: bfloat16 [2, 64, 64, 128], P(None, 'rows'), may hold values from -4 to 4
- second_cache: bfloat16 [2, 64, 64, 128], P(None, 'rows'), may hold values from -4 to 4
- norm1_scale: float32 [128], replicated, may hold values from 0.1 to 1.9
- norm1_shift: float32 [128], replicated, may hold values from -3 to 3
- conv1_weight: bfloat16 [3, 3, 3, 128, 128], replicated, may hold values from -0.109375 to 0.109375
- conv1_bias: float32 [128], replicated, may hold values from -5 to 5
- norm2_scale: float32 [128], replicated, may hold values from 0.1 to 1.9
- norm2_shift: float32 [128], replicated, may hold values from -3 to 3
- conv2_weight: bfloat16 [3, 3, 3, 128, 128], replicated, may hold values from -0.109375 to 0.109375
- conv2_bias: float32 [128], replicated, may hold values from -3 to 3
Outputs:
- block_output: bfloat16 [128, 64, 64, 128], P('section', 'rows')
All inputs are finite; a program needn't handle non-finite values.
Results may differ from a plain program's by a relative error of at most 0.007.
Values may be sent and summed in bfloat16 or wider, within the bound.
A program may use at most 64 MiB of HBM per device.

v0:
```python
import jax
import jax.numpy as jnp
from jax import lax
from jax.sharding import PartitionSpec as P

GROUPS = 32


epsilon = 1e-06


def from_behind(block, axis, distance):
    devices = range(lax.axis_size(axis))
    route = [(i - distance, i) for i in devices if i - distance in devices]
    return lax.ppermute(block, axis, route)


def extended(block, sides, width):
    for axis, dim in sides:
        count = lax.axis_size(axis)
        forward = [(i, i + 1) for i in range(count - 1)]
        backward = [(target, source) for source, target in forward]
        low = lax.ppermute(
            lax.slice_in_dim(block, block.shape[dim] - width, None, axis=dim), axis, forward
        )
        high = lax.ppermute(lax.slice_in_dim(block, 0, width, axis=dim), axis, backward)
        block = jnp.concatenate([low, block, high], axis=dim)
    return block


def group_moments(values):
    frames, row_count, columns, channels = values.shape
    grouped = values.reshape(frames * row_count * columns, GROUPS, channels // GROUPS)
    cells_total = frames * row_count * columns * (channels // GROUPS) * lax.axis_size("rows")
    average = lax.psum(jnp.sum(grouped, axis=(0, 2)), "rows") / cells_total
    centred = grouped - average[None, :, None]
    spread = lax.psum(jnp.sum(centred * centred, axis=(0, 2)), "rows") / cells_total
    return (average, spread)


def apply_norm(values, average, spread, scale, shift):
    frames, row_count, columns, channels = values.shape
    grouped = values.reshape(frames, row_count, columns, GROUPS, channels // GROUPS)
    normal = (grouped - average[:, None]) / jnp.sqrt(spread[:, None] + epsilon)
    normal = normal.reshape(frames, row_count, columns, channels)
    return jax.nn.silu(normal * scale + shift).astype(jnp.bfloat16)


def causal_conv(source, weight, bias):
    frames = source.shape[0] - 2
    row_count = source.shape[1] - 2
    columns = source.shape[2]
    padded = jnp.pad(source, ((0, 0), (0, 0), (1, 1), (0, 0)))
    totals = jnp.zeros((frames, row_count, columns, weight.shape[-1]), jnp.float32)
    for frame_tap in range(3):
        for row_tap in range(3):
            for col_tap in range(3):
                piece = padded[
                    frame_tap : frame_tap + frames,
                    row_tap : row_tap + row_count,
                    col_tap : col_tap + columns,
                ]
                totals = totals + jnp.einsum(
                    "fhwc,cd->fhwd",
                    piece,
                    weight[frame_tap, row_tap, col_tap],
                    preferred_element_type=jnp.float32,
                )
    return totals + bias


def on_device(
    activations,
    first_cache,
    second_cache,
    norm1_scale,
    norm1_shift,
    conv1_weight,
    conv1_bias,
    norm2_scale,
    norm2_shift,
    conv2_weight,
    conv2_bias,
):
    at_start = lax.axis_index("section") == 0
    own_rows = activations.astype(jnp.float32)
    average, spread = group_moments(own_rows)
    entry_block = apply_norm(own_rows, average, spread, norm1_scale, norm1_shift)
    received = from_behind(entry_block[-2:], "section", 1)
    joined = jnp.concatenate([jnp.where(at_start, first_cache, received), entry_block], 0)
    padded = extended(joined, (("rows", 1),), 1)
    middle = causal_conv(padded, conv1_weight, conv1_bias).astype(jnp.bfloat16)
    middle_full = middle.astype(jnp.float32)
    average_two, spread_two = group_moments(middle_full)
    second = apply_norm(middle_full, average_two, spread_two, norm2_scale, norm2_shift)
    received_two = from_behind(second[-2:], "section", 1)
    joined_two = jnp.concatenate([jnp.where(at_start, second_cache, received_two), second], 0)
    padded_two = extended(joined_two, (("rows", 1),), 1)
    final = causal_conv(padded_two, conv2_weight, conv2_bias)
    return (own_rows + final).astype(jnp.bfloat16)


def solution(mesh):
    in_specs = (
        P("section", "rows", None, None),
        P(None, "rows", None, None),
        P(None, "rows", None, None),
        P(),
        P(),
        P(),
        P(),
        P(),
        P(),
        P(),
        P(),
    )
    out_specs = P("section", "rows", None, None)
    return jax.shard_map(
        on_device, mesh=mesh, in_specs=in_specs, out_specs=out_specs, check_vma=False
    )
```

profile of v0, /device:TPU:25, one launch (start us, length us, event | category | flops | bytes accessed | tf_op | source)
XLA Modules:
  0.0 242.9 jit_solution(10656569930719718668)
XLA Ops:
  0.0 1.1 convert_reduce_fusion
  1.4 52.5 %psum.28 = f32[32]{0:T(128)S(1)} all-reduce(f32[32]{0:T(128)S(1)} %reduce_sum.51), channel_id=1, replica_groups=mesh['section'=16,'rows'=32] {'rows'}, use_global_device_ids=true, to_apply=%region_2.0 | all-reduce | flops 32 | bytes 256 | tf_op jit(solution)/shard_map/psum | solution.py:35
  54.0 1.2 fusion.47
  55.4 48.1 %psum.29 = f32[32]{0:T(128)S(1)} all-reduce(f32[32]{0:T(128)S(1)} %reduce_sum.54), channel_id=1, replica_groups=mesh['section'=16,'rows'=32] {'rows'}, use_global_device_ids=true, to_apply=%region_5.6 | all-reduce | flops 32 | bytes 256 | tf_op jit(solution)/shard_map/psum | solution.py:37
  103.7 1.2 multiply_convert_fusion.1
  104.9 3.1 %collective-permute-start = (bf16[2,2,64,128]{3,2,1,0:T(8,128)(2,1)S(1)}, bf16[2,2,64,128]{3,2,1,0:T(8,128)(2,1)S(1)}, u32[]{:S(2)}, u32[]{:S(2)}) collective-permute-start(bf16[2,2,64,128]{3,2,1,0:T(8,128)(2,1)S(1)} %slice.486), channel_id=1, source_target_pairs={{0,32},{32,64},{64,96},{96,128},{128,160},{160,192},{192,224},{224... | collective-permute-start | bytes 196616 | tf_op jit(solution)/shard_map/ppermute | solution.py:15
  108.0 4.0 %collective-permute-done = bf16[2,2,64,128]{3,2,1,0:T(8,128)(2,1)S(1)} collective-permute-done((bf16[2,2,64,128]{3,2,1,0:T(8,128)(2,1)S(1)}, bf16[2,2,64,128]{3,2,1,0:T(8,128)(2,1)S(1)}, u32[]{:S(2)}, u32[]{:S(2)}) %collective-permute-start) | collective-permute-done | bytes 65568 | tf_op jit(solution)/shard_map/ppermute | solution.py:15
  112.1 1.9 collective-permute-start.1
  114.0 3.1 %collective-permute-start.2 = (bf16[10,1,64,128]{3,2,1,0:T(8,128)(2,1)S(1)}, bf16[10,1,64,128]{3,2,1,0:T(8,128)(2,1)S(1)}, u32[]{:S(2)}, u32[]{:S(2)}) collective-permute-start(bf16[10,1,64,128]{3,2,1,0:T(8,128)(2,1)S(1)} %get-tuple-element.8), channel_id=1, source_target_pairs={{1,0},{2,1},{3,2},{4,3},{5,4},{6,5},{7,6},{8,7},{9,8},{10,9},{11,1... | collective-permute-start | bytes 491528 | tf_op jit(solution)/shard_map/ppermute | solution.py:26
  117.1 0.2 fusion.102
  117.5 3.1 %collective-permute-done.2 = bf16[10,1,64,128]{3,2,1,0:T(8,128)(2,1)S(1)} collective-permute-done((bf16[10,1,64,128]{3,2,1,0:T(8,128)(2,1)S(1)}, bf16[10,1,64,128]{3,2,1,0:T(8,128)(2,1)S(1)}, u32[]{:S(2)}, u32[]{:S(2)}) %collective-permute-start.2) | collective-permute-done | bytes 163872 | tf_op jit(solution)/shard_map/ppermute | solution.py:26
  120.6 0.3 fusion.42
  121.0 0.2 fusion.95
  121.2 0.2 fusion.92
  121.4 0.2 fusion.89
  121.6 0.2 fusion.86
  121.8 0.2 fusion.83
  122.0 0.2 fusion.80
  122.3 0.2 fusion.75
  122.5 0.2 fusion.171
  122.9 0.2 convolution_add_fusion.22
  123.1 0.2 fusion.2
  123.6 0.2 fusion.4
  124.0 0.2 fusion.6
  124.3 0.2 fusion.8
  124.7 0.2 fusion.10
  124.9 0.2 fusion.149
  125.1 0.2 fusion.12
  125.3 0.2 convolution_add_fusion.15
  125.6 0.2 convolution_add_fusion.14
  125.8 0.2 convolution_add_fusion.13
  126.0 0.2 fusion.142
  126.2 0.4 copy-done.5
  126.7 0.3 fusion.232
  127.2 43.5 %psum.30 = f32[32]{0:T(128)S(1)} all-reduce(f32[32]{0:T(128)S(1)} %reduce_sum.72), channel_id=1, replica_groups=mesh['section'=16,'rows'=32] {'rows'}, use_global_device_ids=true, to_apply=%region_8.9 | all-reduce | flops 32 | bytes 256 | tf_op jit(solution)/shard_map/psum | solution.py:35
  171.3 47.9 %psum.31 = f32[32]{0:T(128)S(1)} all-reduce(f32[32]{0:T(128)S(1)} %reduce_sum.75), channel_id=1, replica_groups=mesh['section'=16,'rows'=32] {'rows'}, use_global_device_ids=true, to_apply=%region_11.12 | all-reduce | flops 32 | bytes 256 | tf_op jit(solution)/shard_map/psum | solution.py:37
  219.7 2.1 collective-permute-start.3
  221.7 5.2 %collective-permute-done.3 = bf16[2,2,64,128]{3,2,1,0:T(8,128)(2,1)S(1)} collective-permute-done((bf16[2,2,64,128]{3,2,1,0:T(8,128)(2,1)S(1)}, bf16[2,2,64,128]{3,2,1,0:T(8,128)(2,1)S(1)}, u32[]{:S(2)}, u32[]{:S(2)}) %collective-permute-start.3) | collective-permute-done | bytes 65568 | tf_op jit(solution)/shard_map/ppermute | solution.py:15
  227.0 1.9 collective-permute-start.4
  228.9 3.1 %collective-permute-start.5 = (bf16[10,1,64,128]{3,2,1,0:T(8,128)(2,1)S(1)}, bf16[10,1,64,128]{3,2,1,0:T(8,128)(2,1)S(1)}, u32[]{:S(2)}, u32[]{:S(2)}) collective-permute-start(bf16[10,1,64,128]{3,2,1,0:T(8,128)(2,1)S(1)} %get-tuple-element.6), channel_id=1, source_target_pairs={{1,0},{2,1},{3,2},{4,3},{5,4},{6,5},{7,6},{8,7},{9,8},{10,9},{11,1... | collective-permute-start | bytes 491528 | tf_op jit(solution)/shard_map/ppermute | solution.py:26
  232.2 0.2 fusion.101
  232.4 3.1 %collective-permute-done.5 = bf16[10,1,64,128]{3,2,1,0:T(8,128)(2,1)S(1)} collective-permute-done((bf16[10,1,64,128]{3,2,1,0:T(8,128)(2,1)S(1)}, bf16[10,1,64,128]{3,2,1,0:T(8,128)(2,1)S(1)}, u32[]{:S(2)}, u32[]{:S(2)}) %collective-permute-start.5) | collective-permute-done | bytes 163872 | tf_op jit(solution)/shard_map/ppermute | solution.py:26
  235.5 0.3 select_maximum_fusion
  235.9 0.2 fusion.70
  236.1 0.2 fusion.67
  236.3 0.2 fusion.64
  236.5 0.2 fusion.61
  236.7 0.2 fusion.58
  237.0 0.2 fusion.55
  237.2 0.2 fusion.50
  237.6 0.2 convolution_add_fusion.11
  237.8 0.2 convolution_add_fusion.10
  238.0 0.2 fusion.17
  238.3 0.2 fusion.131
  238.5 0.2 fusion.19
  238.9 0.2 fusion.21
  239.1 0.2 fusion.23
  239.6 0.2 fusion.25
  240.0 0.2 fusion.27
  240.3 0.2 convolution_add_fusion.3
  240.5 0.2 convolution_add_fusion.2
  240.7 0.2 convolution_add_fusion.1
  241.2 0.7 copy-done
  241.9 1.0 fusion.34
  (57 shorter events, 4.3 us)
Async XLA Ops:
  0.0 112.0 %copy-start.3 = (bf16[2,2,64,128]{3,2,1,0:T(8,128)(2,1)S(1)}, bf16[2,2,64,128]{3,2,1,0:T(8,128)(2,1)}, u32[]{:S(2)}) copy-start(bf16[2,2,64,128]{3,2,1,0:T(8,128)(2,1)} %param.12) | copy-start | bytes 196612
  54.0 63.1 %copy-start.1 = (bf16[3,3,3,128,128]{4,3,2,1,0:T(8,128)(2,1)S(1)}, bf16[3,3,3,128,128]{4,3,2,1,0:T(8,128)(2,1)}, u32[]{:S(2)}) copy-start(bf16[3,3,3,128,128]{4,3,2,1,0:T(8,128)(2,1)} %param.16) | copy-start | bytes 2654212
  104.9 7.1 %collective-permute-start = (bf16[2,2,64,128]{3,2,1,0:T(8,128)(2,1)S(1)}, bf16[2,2,64,128]{3,2,1,0:T(8,128)(2,1)S(1)}, u32[]{:S(2)}, u32[]{:S(2)}) collective-permute-start(bf16[2,2,64,128]{3,2,1,0:T(8,128)(2,1)S(1)} %slice.486), channel_id=1, source_target_pairs={{0,32},{32,64},{64,96},{96,128},{128,160},{160,192},{192,224},{224... | collective-permute-start | bytes 196616 | tf_op jit(solution)/shard_map/ppermute | solution.py:15
  112.1 5.5 %collective-permute-start.1 = (bf16[10,1,64,128]{3,2,1,0:T(8,128)(2,1)S(1)}, bf16[10,1,64,128]{3,2,1,0:T(8,128)(2,1)S(1)}, u32[]{:S(2)}, u32[]{:S(2)}) collective-permute-start(bf16[10,1,64,128]{3,2,1,0:T(8,128)(2,1)S(1)} %get-tuple-element.7), channel_id=1, source_target_pairs={{0,1},{1,2},{2,3},{3,4},{4,5},{5,6},{6,7},{7,8},{8,9},{9,10},{10,1... | collective-permute-start | bytes 491528 | tf_op jit(solution)/shard_map/ppermute | solution.py:23
  114.0 6.6 %collective-permute-start.2 = (bf16[10,1,64,128]{3,2,1,0:T(8,128)(2,1)S(1)}, bf16[10,1,64,128]{3,2,1,0:T(8,128)(2,1)S(1)}, u32[]{:S(2)}, u32[]{:S(2)}) collective-permute-start(bf16[10,1,64,128]{3,2,1,0:T(8,128)(2,1)S(1)} %get-tuple-element.8), channel_id=1, source_target_pairs={{1,0},{2,1},{3,2},{4,3},{5,4},{6,5},{7,6},{8,7},{9,8},{10,9},{11,1... | collective-permute-start | bytes 491528 | tf_op jit(solution)/shard_map/ppermute | solution.py:26
  126.0 0.7 copy-start.5
  126.7 92.8 %copy-start.6 = (f32[128]{0:T(128)S(1)}, f32[128]{0:T(128)}, u32[]{:S(2)}) copy-start(f32[128]{0:T(128)} %param.19) | copy-start | bytes 1540
  126.7 92.8 %copy-start.7 = (f32[128]{0:T(128)S(1)}, f32[128]{0:T(128)}, u32[]{:S(2)}) copy-start(f32[128]{0:T(128)} %param.18) | copy-start | bytes 1540
  127.0 99.9 %copy-start.4 = (bf16[2,2,64,128]{3,2,1,0:T(8,128)(2,1)S(1)}, bf16[2,2,64,128]{3,2,1,0:T(8,128)(2,1)}, u32[]{:S(2)}) copy-start(bf16[2,2,64,128]{3,2,1,0:T(8,128)(2,1)} %param.13) | copy-start | bytes 196612
  219.4 12.6 %copy-start.2 = (bf16[3,3,3,128,128]{4,3,2,1,0:T(8,128)(2,1)S(1)}, bf16[3,3,3,128,128]{4,3,2,1,0:T(8,128)(2,1)}, u32[]{:S(2)}) copy-start(bf16[3,3,3,128,128]{4,3,2,1,0:T(8,128)(2,1)} %param.20) | copy-start | bytes 2654212
  219.7 7.3 %collective-permute-start.3 = (bf16[2,2,64,128]{3,2,1,0:T(8,128)(2,1)S(1)}, bf16[2,2,64,128]{3,2,1,0:T(8,128)(2,1)S(1)}, u32[]{:S(2)}, u32[]{:S(2)}) collective-permute-start(bf16[2,2,64,128]{3,2,1,0:T(8,128)(2,1)S(1)} %slice.509), channel_id=1, source_target_pairs={{0,32},{32,64},{64,96},{96,128},{128,160},{160,192},{192,224},{224... | collective-permute-start | bytes 196616 | tf_op jit(solution)/shard_map/ppermute | solution.py:15
  227.0 5.5 %collective-permute-start.4 = (bf16[10,1,64,128]{3,2,1,0:T(8,128)(2,1)S(1)}, bf16[10,1,64,128]{3,2,1,0:T(8,128)(2,1)S(1)}, u32[]{:S(2)}, u32[]{:S(2)}) collective-permute-start(bf16[10,1,64,128]{3,2,1,0:T(8,128)(2,1)S(1)} %get-tuple-element.5), channel_id=1, source_target_pairs={{0,1},{1,2},{2,3},{3,4},{4,5},{5,6},{6,7},{7,8},{8,9},{9,10},{10,1... | collective-permute-start | bytes 491528 | tf_op jit(solution)/shard_map/ppermute | solution.py:23
  228.9 6.6 %collective-permute-start.5 = (bf16[10,1,64,128]{3,2,1,0:T(8,128)(2,1)S(1)}, bf16[10,1,64,128]{3,2,1,0:T(8,128)(2,1)S(1)}, u32[]{:S(2)}, u32[]{:S(2)}) collective-permute-start(bf16[10,1,64,128]{3,2,1,0:T(8,128)(2,1)S(1)} %get-tuple-element.6), channel_id=1, source_target_pairs={{1,0},{2,1},{3,2},{4,3},{5,4},{6,5},{7,6},{8,7},{9,8},{10,9},{11,1... | collective-permute-start | bytes 491528 | tf_op jit(solution)/shard_map/ppermute | solution.py:26
  240.9 1.0 copy-start
  240.9 0.9 copy-start.8
where the time goes:
time: 246 us; the launch traced here: 243 us
  blocking collectives  192 us (78%)
  waiting for transfers between devices  15.4 us (6%)
  starting transfers between devices  15.2 us (6%)
  matrix products  12.3 us (5%)
  other arithmetic  5.02 us (2%)
    psum x2, blocking collectives, group_moments(): lax.psum(jnp.sum(centred * centred, axis=(0, 2)), 'rows') / cells_total  96 us
    psum x2, blocking collectives, group_moments(): average = lax.psum(jnp.sum(grouped, axis=(0, 2)), 'rows') / cells_total  96 us
    dot_general x54, matrix products, causal_conv(): jnp.einsum('fhwc,cd->fhwd', piece, weight[frame_tap, row_tap, col_tap], p...  12.3 us
    ppermute x2, waiting for transfers between devices, from_behind(): return lax.ppermute(block, axis, route)  9.18 us
    ppermute x2, waiting for transfers between devices, extended(): lax.ppermute(lax.slice_in_dim(block, 0, width, axis=dim), axis, backward)  6.21 us
    ppermute x2, starting transfers between devices, extended(): lax.ppermute(lax.slice_in_dim(block, 0, width, axis=dim), axis, backward)  6.17 us
    ppermute x2, starting transfers between devices, from_behind(): return lax.ppermute(block, axis, route)  5.17 us
  transfers between devices with their start and end apart: 6, of which 4 were waited for; matrix products, arithmetic and copies ran while one was open for 0% of the time, Pallas kernels for 0%

commit v1 on v0

v1 whole, which is shorter than its diff:
```python
import functools

import jax
import jax.numpy as jnp
from jax import lax
from jax.experimental import pallas as pl
from jax.experimental.pallas import tpu as pltpu
from jax.sharding import PartitionSpec as P

MESH = pl.DeviceIdType.MESH
EPS = 1e-06
F32 = jnp.float32
BF16 = jnp.bfloat16
SPAN, ROWS, COLS, C = 8, 2, 64, 128


def lane_group_sum(x):
    lane = lax.broadcasted_iota(jnp.int32, x.shape, 1)
    x = x + jnp.where(lane % 2 == 0, pltpu.roll(x, 127, 1), pltpu.roll(x, 1, 1))
    return x + jnp.where(lane % 4 < 2, pltpu.roll(x, 126, 1), pltpu.roll(x, 2, 1))


def kernel(
    n_sec,
    n_row,
    acts,
    cache1,
    cache2,
    g1,
    b1,
    w1,
    bias1,
    g2,
    b2,
    w2,
    bias2,
    out,
    xa,
    mid,
    par,
    wb1,
    wb2,
    u,
    pb,
    hl,
    hr,
    pv,
    st,
    mv,
    load_sem,
    w_sem,
    halo_send,
    halo_recv,
    cache_send,
    cache_loc,
    st_send,
    st_recv,
    mv_send,
    mv_recv,
):
    s = lax.axis_index("section")
    r = lax.axis_index("rows")
    first, last = s == 0, s == n_sec - 1
    top, bottom = r == 0, r == n_row - 1
    has_up, has_down = jnp.logical_not(top), jnp.logical_not(bottom)
    has_prev, has_next = jnp.logical_not(first), jnp.logical_not(last)
    both = jnp.logical_and

    def dev(ds, dr):
        return {"section": s + ds, "rows": r + dr}

    barrier = pltpu.get_barrier_semaphore()

    def greet(k, carry):
        pl.semaphore_signal(
            barrier, inc=1, device_id={"section": s, "rows": lax.rem(r + k, n_row)}, device_id_type=MESH
        )
        return carry

    lax.fori_loop(1, n_row, greet, 0)
    near = []
    for ds, cs in ((-1, has_prev), (1, has_next)):
        near.append((ds, 0, cs))
        near.append((ds, -1, both(cs, has_up)))
        near.append((ds, 1, both(cs, has_down)))
    expected = jnp.int32(n_row - 1)
    for ds, dr, cond in near:

        @pl.when(cond)
        def _(ds=ds, dr=dr):
            pl.semaphore_signal(barrier, inc=1, device_id=dev(ds, dr), device_id_type=MESH)

        expected = expected + cond.astype(jnp.int32)

    load_x = pltpu.make_async_copy(acts, xa, load_sem.at[0])
    load_x.start()
    par_loads = []
    for i, ref in enumerate((g1, b1, bias1, g2, b2, bias2)):
        par_loads.append(pltpu.make_async_copy(ref, par.at[i], load_sem.at[1 + i]))
        par_loads[-1].start()
    w_loads = []
    for conv, (w, wb) in enumerate(((w1, wb1), (w2, wb2))):
        for dh in range(3):
            for o in range(2):
                rr = dh + o
                copy = pltpu.make_async_copy(
                    w.at[:, dh],
                    wb.at[:, :, rr * C : (rr + 1) * C, o * C : (o + 1) * C],
                    w_sem.at[conv, dh * 2 + o],
                )
                copy.start()
                w_loads.append((conv, copy))
    for wb in (wb1, wb2):
        wb[:, :, 0:C, C : 2 * C] = jnp.zeros((3, 3, C, C), BF16)
        wb[:, :, 3 * C : 4 * C, 0:C] = jnp.zeros((3, 3, C, C), BF16)

    def halo(conv, src):
        out_copies = []

        def add(idx, cond, a, b, ds, dr):
            out_copies.append(
                (
                    cond,
                    pltpu.make_async_remote_copy(
                        src_ref=a,
                        dst_ref=b,
                        send_sem=halo_send.at[conv, idx],
                        recv_sem=halo_recv.at[conv, idx],
                        device_id=dev(ds, dr),
                        device_id_type=MESH,
                    ),
                )
            )

        tail = pl.ds(SPAN - 2, 2)
        add(0, has_down, src.at[:, 1], hl.at[conv], 0, 1)
        add(1, has_up, src.at[:, 0], hr.at[conv], 0, -1)
        add(2, has_next, src.at[tail], pv.at[conv, :, 1:3], 1, 0)
        add(3, both(has_next, has_down), src.at[tail, 1], pv.at[conv, :, 0], 1, 1)
        add(4, both(has_next, has_up), src.at[tail, 0], pv.at[conv, :, 3], 1, -1)
        return out_copies

    def cache_copies(conv, cache):
        local = pltpu.make_async_copy(cache, pv.at[conv, :, 1:3], cache_loc.at[conv])
        remote = []
        for idx, cond, row, slot, dr in ((3, has_down, 1, 0, 1), (4, has_up, 0, 3, -1)):
            remote.append(
                (
                    cond,
                    pltpu.make_async_remote_copy(
                        src_ref=cache.at[:, row],
                        dst_ref=pv.at[conv, :, slot],
                        send_sem=cache_send.at[conv, idx - 3],
                        recv_sem=halo_recv.at[conv, idx],
                        device_id=dev(0, dr),
                        device_id_type=MESH,
                    ),
                )
            )
        return local, remote

    def start_all(copies, extra=None):
        for cond, copy in copies:

            @pl.when(cond if extra is None else both(cond, extra))
            def _(copy=copy):
                copy.start()

    def wait_send_all(copies, extra=None):
        for cond, copy in copies:

            @pl.when(cond if extra is None else both(cond, extra))
            def _(copy=copy):
                copy.wait_send()

    def stat_copy(conv, k):
        peer = lax.rem(r + k, n_row)
        return pltpu.make_async_remote_copy(
            src_ref=st.at[conv, r],
            dst_ref=st.at[conv, r],
            send_sem=st_send.at[conv],
            recv_sem=st_recv.at[conv],
            device_id={"section": s, "rows": peer},
            device_id_type=MESH,
        )

    def local_stats(conv, load):
        x = load()
        mean = jnp.sum(jnp.sum(x, axis=0), axis=0, keepdims=True) * (1.0 / (SPAN * ROWS * COLS))
        d = x - mean[None]
        m2 = jnp.sum(jnp.sum(d * d, axis=0), axis=0, keepdims=True)
        st[conv, r] = jnp.concatenate([mean, m2], axis=0)

        def send(k, carry):
            stat_copy(conv, k).start()
            return carry

        lax.fori_loop(1, n_row, send, 0)

    def wait_stats(conv):
        bulk = st.at[conv, pl.ds(0, n_row - 1)]
        pltpu.make_async_copy(bulk, bulk, st_recv.at[conv]).wait()

    def wait_stats_sent(conv):
        bulk = st.at[conv, pl.ds(0, n_row - 1)]
        pltpu.make_async_copy(bulk, bulk, st_send.at[conv]).wait()

    def combine(conv, scale):
        means = st[conv, :, 0, :]
        m2s = st[conv, :, 1, :]
        total = jnp.sum(means, axis=0, keepdims=True)
        mean = lane_group_sum(jnp.broadcast_to(total, (8, C)))[0:1] * (1.0 / (4 * n_row))
        d = means - mean
        q = jnp.sum(m2s + (SPAN * ROWS * COLS) * (d * d), axis=0, keepdims=True)
        spread = lane_group_sum(jnp.broadcast_to(q, (8, C)))[0:1] * (1.0 / (4 * SPAN * ROWS * COLS * n_row))
        factor = scale / jnp.sqrt(spread + EPS)
        mv[conv, 0] = jnp.concatenate([mean, factor], axis=0)

    def mv_copy(conv):
        return pltpu.make_async_remote_copy(
            src_ref=mv.at[conv, 0],
            dst_ref=mv.at[conv, 1],
            send_sem=mv_send.at[conv],
            recv_sem=mv_recv.at[conv],
            device_id=dev(1, 0),
            device_id_type=MESH,
        )

    def norm(x, mean, factor, shift):
        v = (x.astype(F32) - mean) * factor + shift
        return (v / (1.0 + jnp.exp(-v))).astype(BF16)

    def fill_own(conv, src, shift):
        mean = mv[conv, 0, 0:1, :]
        factor = mv[conv, 0, 1:2, :]

        def own(f, carry):
            for row in range(2):
                u[f + 2, :, (row + 1) * C : (row + 2) * C] = norm(src[f, row], mean, factor, shift)
            return carry

        lax.fori_loop(0, SPAN, own, 0)
        for idx, cond, ref, rr in ((0, has_up, hl, 0), (1, has_down, hr, 3)):

            @pl.when(cond)
            def _(idx=idx, ref=ref, rr=rr):
                pltpu.make_async_copy(ref.at[conv], ref.at[conv], halo_recv.at[conv, idx]).wait()

                def step(f, carry):
                    u[f + 2, :, rr * C : (rr + 1) * C] = norm(ref[conv, f], mean, factor, shift)
                    return carry

                lax.fori_loop(0, SPAN, step, 0)

    def fill_prev(conv, shift):
        @pl.when(has_prev)
        def _():
            pltpu.make_async_copy(mv.at[conv, 1], mv.at[conv, 1], mv_recv.at[conv]).wait()
            pltpu.make_async_copy(pv.at[conv, :, 1:3], pv.at[conv, :, 1:3], halo_recv.at[conv, 2]).wait()

        @pl.when(first)
        def _():
            pltpu.make_async_copy(pv.at[conv, :, 1:3], pv.at[conv, :, 1:3], cache_loc.at[conv]).wait()

        for idx, cond, slot in ((3, has_up, 0), (4, has_down, 3)):

            @pl.when(cond)
            def _(idx=idx, slot=slot):
                pltpu.make_async_copy(pv.at[conv, :, slot], pv.at[conv, :, slot], halo_recv.at[conv, idx]).wait()

        for slot, cond in ((0, has_up), (1, None), (2, None), (3, has_down)):
            lanes = slice(slot * C, (slot + 1) * C)

            @pl.when(has_prev if cond is None else both(cond, has_prev))
            def _(slot=slot, lanes=lanes):
                mean = mv[conv, 1, 0:1, :]
                factor = mv[conv, 1, 1:2, :]
                for f in range(2):
                    u[f, :, lanes] = norm(pv[conv, f, slot], mean, factor, shift)

            @pl.when(first if cond is None else both(cond, first))
            def _(slot=slot, lanes=lanes):
                for f in range(2):
                    u[f, :, lanes] = pv[conv, f, slot]

    def conv_chunk(wb, f0, count):
        m = count * COLS
        lhs = jnp.concatenate([u[f0 + dt : f0 + dt + count].reshape(m, 4 * C) for dt in range(3)], axis=1)
        for dw in range(3):
            rhs = jnp.concatenate([wb[dt, dw] for dt in range(3)], axis=0)
            pb[dw, f0 * COLS : f0 * COLS + m] = jnp.dot(lhs, rhs, preferred_element_type=F32)

    def gathered(f, bias):
        rows = pl.ds(pl.multiple_of(f * COLS, COLS), COLS)
        col = lax.broadcasted_iota(jnp.int32, (COLS, 2 * C), 0)
        low = jnp.where(col == 0, 0.0, pltpu.roll(pb[0, rows], 1, 0))
        high = jnp.where(col == COLS - 1, 0.0, pltpu.roll(pb[2, rows], COLS - 1, 0))
        y = low + pb[1, rows] + high
        return y[:, 0:C] + bias, y[:, C : 2 * C] + bias

    for cond, rr in ((top, 0), (bottom, 3)):

        @pl.when(cond)
        def _(rr=rr):
            u[:, :, rr * C : (rr + 1) * C] = jnp.zeros((SPAN + 2, COLS, C), BF16)

    pl.semaphore_wait(barrier, expected)

    load_x.wait()
    local_stats(0, lambda: xa[...].astype(F32).reshape(SPAN * ROWS, COLS, C))
    halo1 = halo(0, acts)
    start_all(halo1)
    caches = [cache_copies(0, cache1), cache_copies(1, cache2)]
    for local, remote in caches:

        @pl.when(first)
        def _(local=local):
            local.start()

        start_all(remote, first)
    for copy in par_loads:
        copy.wait()
    for conv, copy in w_loads:
        if conv == 0:
            copy.wait()

    wait_stats(0)
    combine(0, par[0:1])
    send_mv = mv_copy(0)

    @pl.when(has_next)
    def _():
        send_mv.start()

    fill_own(0, xa, par[1:2])
    conv_chunk(wb1, 2, SPAN - 2)
    fill_prev(0, par[1:2])
    conv_chunk(wb1, 0, 2)

    def store_mid(f, carry):
        lo, hi = gathered(f, par[2:3])
        mid[f, 0] = lo.astype(BF16)
        mid[f, 1] = hi.astype(BF16)
        return carry

    lax.fori_loop(0, SPAN, store_mid, 0)

    halo2 = halo(1, mid)
    local_stats(1, lambda: mid[...].astype(F32).reshape(SPAN * ROWS, COLS, C))
    start_all(halo2)
    for conv, copy in w_loads:
        if conv == 1:
            copy.wait()
    wait_send_all(halo1)
    for _, remote in caches:
        wait_send_all(remote, first)
    wait_stats_sent(0)

    @pl.when(has_next)
    def _():
        send_mv.wait_send()

    wait_stats(1)
    combine(1, par[3:4])
    send_mv2 = mv_copy(1)

    @pl.when(has_next)
    def _():
        send_mv2.start()

    fill_own(1, mid, par[4:5])
    conv_chunk(wb2, 2, SPAN - 2)
    fill_prev(1, par[4:5])
    conv_chunk(wb2, 0, 2)

    def store_out(f, carry):
        lo, hi = gathered(f, par[5:6])
        out[f, 0] = (xa[f, 0].astype(F32) + lo).astype(BF16)
        out[f, 1] = (xa[f, 1].astype(F32) + hi).astype(BF16)
        return carry

    lax.fori_loop(0, SPAN, store_out, 0)
    wait_send_all(halo2)
    wait_stats_sent(1)

    @pl.when(has_next)
    def _():
        send_mv2.wait_send()


def solution(mesh):
    n_sec, n_row = mesh.shape["section"], mesh.shape["rows"]

    def step(*args):
        any_spec = pl.BlockSpec(memory_space=pl.ANY)
        return pl.pallas_call(
            functools.partial(kernel, n_sec, n_row),
            out_shape=jax.ShapeDtypeStruct((SPAN, ROWS, COLS, C), BF16),
            in_specs=[any_spec] * 11,
            out_specs=pl.BlockSpec(memory_space=pltpu.VMEM),
            scratch_shapes=[
                pltpu.VMEM((SPAN, ROWS, COLS, C), BF16),
                pltpu.VMEM((SPAN, ROWS, COLS, C), BF16),
                pltpu.VMEM((8, C), F32),
                pltpu.VMEM((3, 3, 4 * C, 2 * C), BF16),
                pltpu.VMEM((3, 3, 4 * C, 2 * C), BF16),
                pltpu.VMEM((SPAN + 2, COLS, 4 * C), BF16),
                pltpu.VMEM((3, SPAN * COLS, 2 * C), F32),
                pltpu.VMEM((2, SPAN, COLS, C), BF16),
                pltpu.VMEM((2, SPAN, COLS, C), BF16),
                pltpu.VMEM((2, 2, 4, COLS, C), BF16),
                pltpu.VMEM((2, n_row, 2, C), F32),
                pltpu.VMEM((2, 2, 2, C), F32),
                pltpu.SemaphoreType.DMA((7,)),
                pltpu.SemaphoreType.DMA((2, 6)),
                pltpu.SemaphoreType.DMA((2, 5)),
                pltpu.SemaphoreType.DMA((2, 5)),
                pltpu.SemaphoreType.DMA((2, 2)),
                pltpu.SemaphoreType.DMA((2,)),
                pltpu.SemaphoreType.DMA((2,)),
                pltpu.SemaphoreType.DMA((2,)),
                pltpu.SemaphoreType.DMA((2,)),
                pltpu.SemaphoreType.DMA((2,)),
            ],
            compiler_params=pltpu.CompilerParams(collective_id=0, has_side_effects=True),
        )(*args)

    rep = P()
    tile = P("section", "rows", None, None)
    cache = P(None, "rows", None, None)
    return jax.shard_map(
        step,
        mesh=mesh,
        in_specs=(tile, cache, cache) + (rep,) * 8,
        out_specs=tile,
        check_vma=False,
    )
```

time: 246 us -> 43.3 us (0.18); the launches traced: 243 us -> 43.2 us
  blocking collectives: 192 us -> 0 us
  Pallas kernels: 0 us -> 41.5 us
  waiting for transfers between devices: 15.4 us -> 0 us
  starting transfers between devices: 15.2 us -> 0 us
  matrix products: 12.3 us -> 0 us
  other arithmetic: 5.02 us -> 0 us
    psum x4 -> x0, blocking collectives: 192 us -> none  [the longest x2 96 us: group_moments(): lax.psum(jnp.sum(centred * centred, axis=(0, 2)), 'rows') / cells_total]
    pallas_call x0 -> x1, Pallas kernels: none -> 41.5 us  [step(): pl.pallas_call(functools.partial(kernel, n_sec, n_row), out_shape=jax.Sha...]
    ppermute x6 -> x0, waiting for transfers between devices: 15.4 us -> none  [the longest x2 9.18 us: from_behind(): return lax.ppermute(block, axis, route)]
    ppermute x6 -> x0, starting transfers between devices: 15.2 us -> none  [the longest x2 6.17 us: extended(): lax.ppermute(lax.slice_in_dim(block, 0, width, axis=dim), axis, backward)]
    dot_general x54 -> x0, matrix products: 12.3 us -> none  [causal_conv(): jnp.einsum('fhwc,cd->fhwd', piece, weight[frame_tap, row_tap, col_tap], p...]
    reduce_sum x7 -> x0, other arithmetic: 2.92 us -> none  [the longest x4 1.56 us: group_moments(): jnp.sum(centred * centred, axis=(0, 2))]
  transfers between devices with their start and end apart: 6 -> 0, of which waited for: 4 -> 0; matrix products, arithmetic and copies ran while one was open for 0% -> 0% of each run, Pallas kernels for 0% -> 0%
where the time goes in v1:
time: 43.3 us; the launch traced here: 43.2 us
  Pallas kernels  41.5 us (96%)
  local copies, waits for them, and re-layouts  1.67 us (4%)
    pallas_call x1, Pallas kernels, step(): pl.pallas_call(functools.partial(kernel, n_sec, n_row), out_shape=jax.Sha...  41.5 us
    unnamed x1, local copies, waits for them, and re-layouts  1.67 us

profile of v1, /device:TPU:25, one launch (start us, length us, event | category | flops | bytes accessed | tf_op | source)
XLA Modules:
  0.0 43.2 jit_solution(17694650973024486820)
XLA Ops:
  0.0 41.5 %shard_map.109 = bf16[8,2,64,128]{3,2,1,0:T(8,128)(2,1)} custom-call(bf16[8,2,64,128]{3,2,1,0:T(8,128)(2,1)} %acts.1, bf16[2,2,64,128]{3,2,1,0:T(8,128)(2,1)} %cache1.1, bf16[2,2,64,128]{3,2,1,0:T(8,128)(2,1)} %cache2.1, f32[128]{0:T(128)} %g1.1, f32[128]{0:T(128)} %b1.1, bf16[3,3,3,128,128]{4,3,2,1,0:T(8,128)(2,1)} %w1.1, f32[128]{0:T(128)} %bias1.1, ...), custom_call_target="tpu_custom_call" | custom-call | tf_op jit(solution)/shard_map/pallas_call | solution.py:396
  41.5 1.7 %copy.13 = bf16[8,2,64,128]{3,2,1,0:T(8,128)(2,1)} copy(bf16[8,2,64,128]{3,2,1,0:T(8,128)(2,1)} %shard_map.109) | data formatting | bytes 524288

commit v2 on v1

--- a/solution.py
+++ b/solution.py
@@ -69,15 +69,30 @@
     def dev(ds, dr):
         return {"section": s + ds, "rows": r + dr}
 
+    load_x = pltpu.make_async_copy(acts, xa, load_sem.at[0])
+    load_x.start()
+
     barrier = pltpu.get_barrier_semaphore()
 
-    def greet(k, carry):
-        pl.semaphore_signal(
-            barrier, inc=1, device_id={"section": s, "rows": lax.rem(r + k, n_row)}, device_id_type=MESH
-        )
-        return carry
-
-    lax.fori_loop(1, n_row, greet, 0)
+    def row_peer(k):
+        peer = r + k
+        return jnp.where(peer >= n_row, peer - n_row, peer)
+
+    def far_first(body):
+        half = n_row // 2
+        body(row_peer(half))
+
+        def pair(k, carry):
+            body(row_peer(half + k))
+            body(row_peer(half - k))
+            return carry
+
+        lax.fori_loop(1, half, pair, 0)
+
+    def greet(peer):
+        pl.semaphore_signal(barrier, inc=1, device_id={"section": s, "rows": peer}, device_id_type=MESH)
+
+    far_first(greet)
     near = []
     for ds, cs in ((-1, has_prev), (1, has_next)):
         near.append((ds, 0, cs))
@@ -92,8 +107,6 @@
 
         expected = expected + cond.astype(jnp.int32)
 
-    load_x = pltpu.make_async_copy(acts, xa, load_sem.at[0])
-    load_x.start()
     par_loads = []
     for i, ref in enumerate((g1, b1, bias1, g2, b2, bias2)):
         par_loads.append(pltpu.make_async_copy(ref, par.at[i], load_sem.at[1 + i]))
@@ -110,9 +123,6 @@
                 )
                 copy.start()
                 w_loads.append((conv, copy))
-    for wb in (wb1, wb2):
-        wb[:, :, 0:C, C : 2 * C] = jnp.zeros((3, 3, C, C), BF16)
-        wb[:, :, 3 * C : 4 * C, 0:C] = jnp.zeros((3, 3, C, C), BF16)
 
     def halo(conv, src):
         out_copies = []
@@ -173,8 +183,7 @@
             def _(copy=copy):
                 copy.wait_send()
 
-    def stat_copy(conv, k):
-        peer = lax.rem(r + k, n_row)
+    def stat_copy(conv, peer):
         return pltpu.make_async_remote_copy(
             src_ref=st.at[conv, r],
             dst_ref=st.at[conv, r],
@@ -184,18 +193,13 @@
             device_id_type=MESH,
         )
 
-    def local_stats(conv, load):
-        x = load()
-        mean = jnp.sum(jnp.sum(x, axis=0), axis=0, keepdims=True) * (1.0 / (SPAN * ROWS * COLS))
-        d = x - mean[None]
+    n_local = SPAN * ROWS * COLS
+
+    def send_stats(conv, mean, src):
+        d = src[...].astype(F32).reshape(SPAN * ROWS, COLS, C) - mean[None]
         m2 = jnp.sum(jnp.sum(d * d, axis=0), axis=0, keepdims=True)
         st[conv, r] = jnp.concatenate([mean, m2], axis=0)
-
-        def send(k, carry):
-            stat_copy(conv, k).start()
-            return carry
-
-        lax.fori_loop(1, n_row, send, 0)
+        far_first(lambda peer: stat_copy(conv, peer).start())
 
     def wait_stats(conv):
         bulk = st.at[conv, pl.ds(0, n_row - 1)]
@@ -213,7 +217,7 @@
         d = means - mean
         q = jnp.sum(m2s + (SPAN * ROWS * COLS) * (d * d), axis=0, keepdims=True)
         spread = lane_group_sum(jnp.broadcast_to(q, (8, C)))[0:1] * (1.0 / (4 * SPAN * ROWS * COLS * n_row))
-        factor = scale / jnp.sqrt(spread + EPS)
+        factor = 0.5 * scale / jnp.sqrt(spread + EPS)
         mv[conv, 0] = jnp.concatenate([mean, factor], axis=0)
 
     def mv_copy(conv):
@@ -227,32 +231,25 @@
         )
 
     def norm(x, mean, factor, shift):
-        v = (x.astype(F32) - mean) * factor + shift
-        return (v / (1.0 + jnp.exp(-v))).astype(BF16)
-
-    def fill_own(conv, src, shift):
+        h = (x.astype(F32) - mean) * factor + shift
+        return h + h * jnp.tanh(h)
+
+    def wait_halo(conv, idx, ref, cond):
+        @pl.when(cond)
+        def _():
+            pltpu.make_async_copy(ref, ref, halo_recv.at[conv, idx]).wait()
+
+    def fill(conv, src, shift, frames):
         mean = mv[conv, 0, 0:1, :]
         factor = mv[conv, 0, 1:2, :]
-
-        def own(f, carry):
+        for f in frames:
             for row in range(2):
-                u[f + 2, :, (row + 1) * C : (row + 2) * C] = norm(src[f, row], mean, factor, shift)
-            return carry
-
-        lax.fori_loop(0, SPAN, own, 0)
-        for idx, cond, ref, rr in ((0, has_up, hl, 0), (1, has_down, hr, 3)):
-
-            @pl.when(cond)
-            def _(idx=idx, ref=ref, rr=rr):
-                pltpu.make_async_copy(ref.at[conv], ref.at[conv], halo_recv.at[conv, idx]).wait()
-
-                def step(f, carry):
-                    u[f + 2, :, rr * C : (rr + 1) * C] = norm(ref[conv, f], mean, factor, shift)
-                    return carry
-
-                lax.fori_loop(0, SPAN, step, 0)
-
-    def fill_prev(conv, shift):
+                u[f + 2, :, (row + 1) * C : (row + 2) * C] = norm(src[f, row], mean, factor, shift).astype(BF16)
+            for cond, ref, rr in ((has_up, hl, 0), (has_down, hr, 3)):
+                y = jnp.where(cond, norm(ref[conv, f], mean, factor, shift), 0.0)
+                u[f + 2, :, rr * C : (rr + 1) * C] = y.astype(BF16)
+
+    def wait_prev(conv):
         @pl.when(has_prev)
         def _():
             pltpu.make_async_copy(mv.at[conv, 1], mv.at[conv, 1], mv_recv.at[conv]).wait()
@@ -262,52 +259,61 @@
         def _():
             pltpu.make_async_copy(pv.at[conv, :, 1:3], pv.at[conv, :, 1:3], cache_loc.at[conv]).wait()
 
-        for idx, cond, slot in ((3, has_up, 0), (4, has_down, 3)):
-
-            @pl.when(cond)
-            def _(idx=idx, slot=slot):
-                pltpu.make_async_copy(pv.at[conv, :, slot], pv.at[conv, :, slot], halo_recv.at[conv, idx]).wait()
-
-        for slot, cond in ((0, has_up), (1, None), (2, None), (3, has_down)):
-            lanes = slice(slot * C, (slot + 1) * C)
-
-            @pl.when(has_prev if cond is None else both(cond, has_prev))
-            def _(slot=slot, lanes=lanes):
-                mean = mv[conv, 1, 0:1, :]
-                factor = mv[conv, 1, 1:2, :]
-                for f in range(2):
-                    u[f, :, lanes] = norm(pv[conv, f, slot], mean, factor, shift)
-
-            @pl.when(first if cond is None else both(cond, first))
-            def _(slot=slot, lanes=lanes):
-                for f in range(2):
-                    u[f, :, lanes] = pv[conv, f, slot]
-
-    def conv_chunk(wb, f0, count):
-        m = count * COLS
-        lhs = jnp.concatenate([u[f0 + dt : f0 + dt + count].reshape(m, 4 * C) for dt in range(3)], axis=1)
-        for dw in range(3):
-            rhs = jnp.concatenate([wb[dt, dw] for dt in range(3)], axis=0)
-            pb[dw, f0 * COLS : f0 * COLS + m] = jnp.dot(lhs, rhs, preferred_element_type=F32)
+        wait_halo(conv, 3, pv.at[conv, :, 0], has_up)
+        wait_halo(conv, 4, pv.at[conv, :, 3], has_down)
+
+    def fill_prev(conv, shift):
+        mean = mv[conv, 1, 0:1, :]
+        factor = mv[conv, 1, 1:2, :]
+        for f in range(2):
+            for slot, cond in ((0, has_up), (1, None), (2, None), (3, has_down)):
+                raw = pv[conv, f, slot]
+                y = jnp.where(first, raw.astype(F32), norm(raw, mean, factor, shift))
+                if cond is not None:
+                    y = jnp.where(cond, y, 0.0)
+                u[f, :, slot * C : (slot + 1) * C] = y.astype(BF16)
+
+    half_rows = SPAN // 2 * COLS
+    mid_k = 6 * C
+
+    def conv_half(wb, half):
+        f0 = half * (SPAN // 2)
+        rows = slice(half * half_rows, (half + 1) * half_rows)
+        lhs = jnp.concatenate(
+            [u[f0 + dt : f0 + dt + SPAN // 2].reshape(half_rows, 4 * C) for dt in range(3)], axis=1
+        )
+        rhs = [jnp.concatenate([wb[dt, dw] for dt in range(3)], axis=0) for dw in range(3)]
+        pb[0, rows] = jnp.dot(lhs, rhs[0], preferred_element_type=F32)
+        pb[2, rows] = jnp.dot(lhs, rhs[2], preferred_element_type=F32)
+        pb[1, rows] = jnp.dot(lhs[:, :mid_k], rhs[1][:mid_k], preferred_element_type=F32)
+        pb[3, rows] = jnp.dot(lhs[:, mid_k:], rhs[1][mid_k:], preferred_element_type=F32)
 
     def gathered(f, bias):
-        rows = pl.ds(pl.multiple_of(f * COLS, COLS), COLS)
+        rows = slice(f * COLS, (f + 1) * COLS)
         col = lax.broadcasted_iota(jnp.int32, (COLS, 2 * C), 0)
         low = jnp.where(col == 0, 0.0, pltpu.roll(pb[0, rows], 1, 0))
         high = jnp.where(col == COLS - 1, 0.0, pltpu.roll(pb[2, rows], COLS - 1, 0))
-        y = low + pb[1, rows] + high
+        y = (low + pb[1, rows]) + (pb[3, rows] + high)
         return y[:, 0:C] + bias, y[:, C : 2 * C] + bias
 
-    for cond, rr in ((top, 0), (bottom, 3)):
-
-        @pl.when(cond)
-        def _(rr=rr):
-            u[:, :, rr * C : (rr + 1) * C] = jnp.zeros((SPAN + 2, COLS, C), BF16)
-
+    def gather_mid(frames, total):
+        for f in frames:
+            for row, y in enumerate(gathered(f, par[2:3])):
+                y = y.astype(BF16)
+                mid[f, row] = y
+                total = total + y.astype(F32)
+        return total
+
+    def gather_out(frames):
+        for f in frames:
+            for row, y in enumerate(gathered(f, par[5:6])):
+                out[f, row] = (xa[f, row].astype(F32) + y).astype(BF16)
+
+    load_x.wait()
+    x = xa[...].astype(F32).reshape(SPAN * ROWS, COLS, C)
+    mean = jnp.sum(jnp.sum(x, axis=0), axis=0, keepdims=True) * (1.0 / n_local)
     pl.semaphore_wait(barrier, expected)
-
-    load_x.wait()
-    local_stats(0, lambda: xa[...].astype(F32).reshape(SPAN * ROWS, COLS, C))
+    send_stats(0, mean, xa)
     halo1 = halo(0, acts)
     start_all(halo1)
     caches = [cache_copies(0, cache1), cache_copies(1, cache2)]
@@ -318,39 +324,42 @@
             local.start()
 
         start_all(remote, first)
+    for wb in (wb1, wb2):
+        wb[:, :, 0:C, C : 2 * C] = jnp.zeros((3, 3, C, C), BF16)
+        wb[:, :, 3 * C : 4 * C, 0:C] = jnp.zeros((3, 3, C, C), BF16)
     for copy in par_loads:
         copy.wait()
     for conv, copy in w_loads:
-        if conv == 0:
-            copy.wait()
-
-    wait_stats(0)
-    combine(0, par[0:1])
-    send_mv = mv_copy(0)
-
-    @pl.when(has_next)
-    def _():
-        send_mv.start()
-
-    fill_own(0, xa, par[1:2])
-    conv_chunk(wb1, 2, SPAN - 2)
-    fill_prev(0, par[1:2])
-    conv_chunk(wb1, 0, 2)
-
-    def store_mid(f, carry):
-        lo, hi = gathered(f, par[2:3])
-        mid[f, 0] = lo.astype(BF16)
-        mid[f, 1] = hi.astype(BF16)
-        return carry
-
-    lax.fori_loop(0, SPAN, store_mid, 0)
-
+        copy.wait()
+
+    early, late = range(2, SPAN), range(2)
+
+    def stage(conv, src, scale, shift):
+        wait_stats(conv)
+        combine(conv, scale)
+        send_mv = mv_copy(conv)
+
+        @pl.when(has_next)
+        def _():
+            send_mv.start()
+
+        wait_halo(conv, 0, hl.at[conv], has_up)
+        wait_halo(conv, 1, hr.at[conv], has_down)
+        fill(conv, src, shift, early)
+        conv_half((wb1, wb2)[conv], 1)
+        fill(conv, src, shift, late)
+        wait_prev(conv)
+        fill_prev(conv, shift)
+        conv_half((wb1, wb2)[conv], 0)
+        return send_mv
+
+    send_mv = stage(0, xa, par[0:1], 0.5 * par[1:2])
+    total = gather_mid(range(4, SPAN), jnp.zeros((COLS, C), F32))
+    total = gather_mid(range(4), total)
+
+    send_stats(1, jnp.sum(total, axis=0, keepdims=True) * (1.0 / n_local), mid)
     halo2 = halo(1, mid)
-    local_stats(1, lambda: mid[...].astype(F32).reshape(SPAN * ROWS, COLS, C))
     start_all(halo2)
-    for conv, copy in w_loads:
-        if conv == 1:
-            copy.wait()
     wait_send_all(halo1)
     for _, remote in caches:
         wait_send_all(remote, first)
@@ -360,26 +369,9 @@
     def _():
         send_mv.wait_send()
 
-    wait_stats(1)
-    combine(1, par[3:4])
-    send_mv2 = mv_copy(1)
-
-    @pl.when(has_next)
-    def _():
-        send_mv2.start()
-
-    fill_own(1, mid, par[4:5])
-    conv_chunk(wb2, 2, SPAN - 2)
-    fill_prev(1, par[4:5])
-    conv_chunk(wb2, 0, 2)
-
-    def store_out(f, carry):
-        lo, hi = gathered(f, par[5:6])
-        out[f, 0] = (xa[f, 0].astype(F32) + lo).astype(BF16)
-        out[f, 1] = (xa[f, 1].astype(F32) + hi).astype(BF16)
-        return carry
-
-    lax.fori_loop(0, SPAN, store_out, 0)
+    send_mv2 = stage(1, mid, par[3:4], 0.5 * par[4:5])
+    gather_out(range(4, SPAN))
+    gather_out(range(4))
     wait_send_all(halo2)
     wait_stats_sent(1)
 
@@ -405,7 +397,7 @@
                 pltpu.VMEM((3, 3, 4 * C, 2 * C), BF16),
                 pltpu.VMEM((3, 3, 4 * C, 2 * C), BF16),
                 pltpu.VMEM((SPAN + 2, COLS, 4 * C), BF16),
-                pltpu.VMEM((3, SPAN * COLS, 2 * C), F32),
+                pltpu.VMEM((4, SPAN * COLS, 2 * C), F32),
                 pltpu.VMEM((2, SPAN, COLS, C), BF16),
                 pltpu.VMEM((2, SPAN, COLS, C), BF16),
                 pltpu.VMEM((2, 2, 4, COLS, C), BF16),

time: 43.3 us -> 41.2 us (0.952); the launches traced: 43.2 us -> 40.5 us
  Pallas kernels: 41.5 us -> 38.8 us
    pallas_call x1, Pallas kernels: 41.5 us -> 38.8 us  [step(): pl.pallas_call(functools.partial(kernel, n_sec, n_row), out_shape=jax.Sha...]
where the time goes in v2:
time: 41.2 us; the launch traced here: 40.5 us
  Pallas kernels  38.8 us (94%)
  local copies, waits for them, and re-layouts  1.67 us (4%)
    pallas_call x1, Pallas kernels, step(): pl.pallas_call(functools.partial(kernel, n_sec, n_row), out_shape=jax.Sha...  38.8 us
    unnamed x1, local copies, waits for them, and re-layouts  1.67 us

profile of v2, /device:TPU:25, one launch (start us, length us, event | category | flops | bytes accessed | tf_op | source)
XLA Modules:
  0.0 40.5 jit_solution(3276673128494652654)
XLA Ops:
  0.0 38.8 %shard_map.109 = bf16[8,2,64,128]{3,2,1,0:T(8,128)(2,1)} custom-call(bf16[8,2,64,128]{3,2,1,0:T(8,128)(2,1)} %acts.1, bf16[2,2,64,128]{3,2,1,0:T(8,128)(2,1)} %cache1.1, bf16[2,2,64,128]{3,2,1,0:T(8,128)(2,1)} %cache2.1, f32[128]{0:T(128)} %g1.1, f32[128]{0:T(128)} %b1.1, bf16[3,3,3,128,128]{4,3,2,1,0:T(8,128)(2,1)} %w1.1, f32[128]{0:T(128)} %bias1.1, ...), custom_call_target="tpu_custom_call" | custom-call | tf_op jit(solution)/shard_map/pallas_call | solution.py:388
  38.8 1.7 %copy.13 = bf16[8,2,64,128]{3,2,1,0:T(8,128)(2,1)} copy(bf16[8,2,64,128]{3,2,1,0:T(8,128)(2,1)} %shard_map.109) | data formatting | bytes 524288

commit v3 on v2

--- a/solution.py
+++ b/solution.py
@@ -45,7 +45,9 @@
     hl,
     hr,
     pv,
-    st,
+    win,
+    part,
+    full,
     mv,
     load_sem,
     w_sem,
@@ -53,10 +55,13 @@
     halo_recv,
     cache_send,
     cache_loc,
-    st_send,
-    st_recv,
-    mv_send,
-    mv_recv,
+    win_send,
+    win_recv,
+    part_send,
+    part_recv,
+    full_send,
+    full_recv,
+    go,
 ):
     s = lax.axis_index("section")
     r = lax.axis_index("rows")
@@ -72,39 +77,43 @@
     load_x = pltpu.make_async_copy(acts, xa, load_sem.at[0])
     load_x.start()
 
+    ring = n_row // 2
+    reach = ring // 4
+    chip, core = lax.div(r, 2), lax.rem(r, 2)
+
+    def at_chip(offset, which):
+        c = chip + offset
+        c = jnp.where(c >= ring, c - ring, jnp.where(c < 0, c + ring, c))
+        return c * 2 + which
+
+    def window(body):
+        for j in range(reach, 0, -1):
+            for offset in (j, -j):
+                for which in range(2):
+                    body(offset, at_chip(offset, which))
+        body(0, chip * 2 + 1 - core)
+
     barrier = pltpu.get_barrier_semaphore()
 
-    def row_peer(k):
-        peer = r + k
-        return jnp.where(peer >= n_row, peer - n_row, peer)
-
-    def far_first(body):
-        half = n_row // 2
-        body(row_peer(half))
-
-        def pair(k, carry):
-            body(row_peer(half + k))
-            body(row_peer(half - k))
-            return carry
-
-        lax.fori_loop(1, half, pair, 0)
-
-    def greet(peer):
-        pl.semaphore_signal(barrier, inc=1, device_id={"section": s, "rows": peer}, device_id_type=MESH)
-
-    far_first(greet)
-    near = []
-    for ds, cs in ((-1, has_prev), (1, has_next)):
-        near.append((ds, 0, cs))
-        near.append((ds, -1, both(cs, has_up)))
-        near.append((ds, 1, both(cs, has_down)))
-    expected = jnp.int32(n_row - 1)
-    for ds, dr, cond in near:
+    def greet(ds, peer):
+        pl.semaphore_signal(
+            barrier, inc=1, device_id={"section": s + ds, "rows": peer}, device_id_type=MESH
+        )
+
+    window(lambda offset, peer: greet(0, peer))
+    for ds, dr, cond in (
+        (-1, -1, both(has_prev, has_up)),
+        (-1, 0, has_prev),
+        (-1, 1, both(has_prev, has_down)),
+        (1, 0, has_next),
+    ):
 
         @pl.when(cond)
         def _(ds=ds, dr=dr):
-            pl.semaphore_signal(barrier, inc=1, device_id=dev(ds, dr), device_id_type=MESH)
-
+            greet(ds, r + dr)
+
+    expected = jnp.int32(2 * (2 * reach + 1) - 1) + has_prev.astype(jnp.int32)
+    for cond in (has_next, both(has_next, has_up), both(has_next, has_down)):
         expected = expected + cond.astype(jnp.int32)
 
     par_loads = []
@@ -183,52 +192,115 @@
             def _(copy=copy):
                 copy.wait_send()
 
-    def stat_copy(conv, peer):
-        return pltpu.make_async_remote_copy(
-            src_ref=st.at[conv, r],
-            dst_ref=st.at[conv, r],
-            send_sem=st_send.at[conv],
-            recv_sem=st_recv.at[conv],
-            device_id={"section": s, "rows": peer},
+    n_local = SPAN * ROWS * COLS
+    n_win, n_fwd, n_bwd = 2 * (2 * reach + 1), 2 * reach, 2 * (reach - 1)
+
+    def send(src, dst, send_sem, recv_sem, ds, peer):
+        pltpu.make_async_remote_copy(
+            src_ref=src,
+            dst_ref=dst,
+            send_sem=send_sem,
+            recv_sem=recv_sem,
+            device_id={"section": s + ds, "rows": peer},
             device_id_type=MESH,
-        )
-
-    n_local = SPAN * ROWS * COLS
-
-    def send_stats(conv, mean, src):
+        ).start()
+
+    def bulk_wait(ref, sem):
+        pltpu.make_async_copy(ref, ref, sem).wait()
+
+    def local_stats(mean, src):
         d = src[...].astype(F32).reshape(SPAN * ROWS, COLS, C) - mean[None]
         m2 = jnp.sum(jnp.sum(d * d, axis=0), axis=0, keepdims=True)
-        st[conv, r] = jnp.concatenate([mean, m2], axis=0)
-        far_first(lambda peer: stat_copy(conv, peer).start())
-
-    def wait_stats(conv):
-        bulk = st.at[conv, pl.ds(0, n_row - 1)]
-        pltpu.make_async_copy(bulk, bulk, st_recv.at[conv]).wait()
-
-    def wait_stats_sent(conv):
-        bulk = st.at[conv, pl.ds(0, n_row - 1)]
-        pltpu.make_async_copy(bulk, bulk, st_send.at[conv]).wait()
-
-    def combine(conv, scale):
-        means = st[conv, :, 0, :]
-        m2s = st[conv, :, 1, :]
-        total = jnp.sum(means, axis=0, keepdims=True)
-        mean = lane_group_sum(jnp.broadcast_to(total, (8, C)))[0:1] * (1.0 / (4 * n_row))
-        d = means - mean
-        q = jnp.sum(m2s + (SPAN * ROWS * COLS) * (d * d), axis=0, keepdims=True)
-        spread = lane_group_sum(jnp.broadcast_to(q, (8, C)))[0:1] * (1.0 / (4 * SPAN * ROWS * COLS * n_row))
-        factor = 0.5 * scale / jnp.sqrt(spread + EPS)
-        mv[conv, 0] = jnp.concatenate([mean, factor], axis=0)
-
-    def mv_copy(conv):
-        return pltpu.make_async_remote_copy(
-            src_ref=mv.at[conv, 0],
-            dst_ref=mv.at[conv, 1],
-            send_sem=mv_send.at[conv],
-            recv_sem=mv_recv.at[conv],
-            device_id=dev(1, 0),
-            device_id_type=MESH,
+        return jnp.concatenate([mean, m2], axis=0)
+
+    def merged(parts, count, size):
+        mean = jnp.sum(parts[:, 0:1, :], axis=0) * (1.0 / count)
+        d = parts[:, 0:1, :] - mean[None]
+        m2 = jnp.sum(parts[:, 1:2, :] + size * (d * d), axis=0)
+        return jnp.concatenate([mean, m2], axis=0)
+
+    def finish(slot, pieces, scale):
+        mean = sum(count * jnp.sum(p[:, 0, :], axis=0, keepdims=True) for p, count in pieces)
+        mean = lane_group_sum(jnp.broadcast_to(mean, (8, C)))[0:1] * (1.0 / (4 * n_row))
+        q = jnp.zeros((1, C), F32)
+        for p, count in pieces:
+            d = p[:, 0, :] - mean
+            q = q + jnp.sum(p[:, 1, :] + (count * n_local) * (d * d), axis=0, keepdims=True)
+        spread = lane_group_sum(jnp.broadcast_to(q, (8, C)))[0:1] * (1.0 / (4 * n_local * n_row))
+        mv[slot] = jnp.concatenate([mean, 0.5 * scale / jnp.sqrt(spread + EPS)], axis=0)
+
+    def first_exchange(mean):
+        mine = 2 * reach + core
+        win[mine] = local_stats(mean, xa)
+        window(
+            lambda offset, peer: send(
+                win.at[mine], win.at[2 * (reach - offset) + core], win_send, win_recv, 0, peer
+            )
         )
+
+    def second_hop():
+        bulk_wait(win.at[pl.ds(0, n_win - 1)], win_recv)
+        part[0, 0] = merged(win[...], n_win, n_local)
+        part[0, 1] = merged(win[n_win - n_fwd :], n_fwd, n_local)
+        if n_bwd:
+            part[0, 2] = merged(win[2 : 2 + n_bwd], n_bwd, n_local)
+        jobs = [(1, at_chip(-reach, core))]
+        if n_bwd:
+            jobs.append((2, at_chip(reach, core)))
+        for i, peer in jobs:
+            send(part.at[0, i], part.at[1, i], part_send.at[0], part_recv.at[0], 0, peer)
+
+        @pl.when(has_next)
+        def _():
+            pl.semaphore_wait(go.at[0], 1)
+            for i, peer in jobs + [(0, r)]:
+                send(part.at[0, i], part.at[2, i], part_send.at[1], part_recv.at[1], 1, peer)
+
+        n_jobs = len(jobs)
+        bulk_wait(part.at[1, pl.ds(0, n_jobs)], part_recv.at[0])
+
+        @pl.when(has_prev)
+        def _():
+            pl.semaphore_signal(go.at[1], inc=1, device_id=dev(-1, 0), device_id_type=MESH)
+
+        return n_jobs
+
+    def pieces_of(own):
+        out_pieces = [(win[...], 1)] if own else [(part[2, 0:1], n_win)]
+        out_pieces.append((part[1 if own else 2, 1:2], n_fwd))
+        if n_bwd:
+            out_pieces.append((part[1 if own else 2, 2:3], n_bwd))
+        return out_pieces
+
+    def second_exchange(mean):
+        full[0, r] = local_stats(mean, mid)
+
+        @pl.when(has_next)
+        def _():
+            pl.semaphore_wait(go.at[1], 1)
+
+        def one(offset):
+            peer = r + offset
+            peer = jnp.where(peer >= n_row, peer - n_row, peer)
+            send(full.at[0, r], full.at[0, r], full_send.at[0], full_recv.at[0], 0, peer)
+
+            @pl.when(has_next)
+            def _():
+                send(full.at[0, r], full.at[1, r], full_send.at[1], full_recv.at[1], 1, peer)
+
+        half = n_row // 2
+        one(half)
+
+        def pair(k, carry):
+            one(half + k)
+            one(half - k)
+            return carry
+
+        lax.fori_loop(1, half, pair, 0)
+
+        @pl.when(has_next)
+        def _():
+            send(full.at[0, r], full.at[1, r], full_send.at[1], full_recv.at[1], 1, r)
 
     def norm(x, mean, factor, shift):
         h = (x.astype(F32) - mean) * factor + shift
@@ -240,8 +312,8 @@
             pltpu.make_async_copy(ref, ref, halo_recv.at[conv, idx]).wait()
 
     def fill(conv, src, shift, frames):
-        mean = mv[conv, 0, 0:1, :]
-        factor = mv[conv, 0, 1:2, :]
+        mean = mv[0, 0:1, :]
+        factor = mv[0, 1:2, :]
         for f in frames:
             for row in range(2):
                 u[f + 2, :, (row + 1) * C : (row + 2) * C] = norm(src[f, row], mean, factor, shift).astype(BF16)
@@ -249,10 +321,13 @@
                 y = jnp.where(cond, norm(ref[conv, f], mean, factor, shift), 0.0)
                 u[f + 2, :, rr * C : (rr + 1) * C] = y.astype(BF16)
 
-    def wait_prev(conv):
+    def wait_prev(conv, n_jobs):
         @pl.when(has_prev)
         def _():
-            pltpu.make_async_copy(mv.at[conv, 1], mv.at[conv, 1], mv_recv.at[conv]).wait()
+            if conv == 0:
+                bulk_wait(part.at[2, pl.ds(0, n_jobs + 1)], part_recv.at[1])
+            else:
+                bulk_wait(full.at[1], full_recv.at[1])
             pltpu.make_async_copy(pv.at[conv, :, 1:3], pv.at[conv, :, 1:3], halo_recv.at[conv, 2]).wait()
 
         @pl.when(first)
@@ -263,8 +338,8 @@
         wait_halo(conv, 4, pv.at[conv, :, 3], has_down)
 
     def fill_prev(conv, shift):
-        mean = mv[conv, 1, 0:1, :]
-        factor = mv[conv, 1, 1:2, :]
+        mean = mv[1, 0:1, :]
+        factor = mv[1, 1:2, :]
         for f in range(2):
             for slot, cond in ((0, has_up), (1, None), (2, None), (3, has_down)):
                 raw = pv[conv, f, slot]
@@ -285,15 +360,16 @@
         rhs = [jnp.concatenate([wb[dt, dw] for dt in range(3)], axis=0) for dw in range(3)]
         pb[0, rows] = jnp.dot(lhs, rhs[0], preferred_element_type=F32)
         pb[2, rows] = jnp.dot(lhs, rhs[2], preferred_element_type=F32)
-        pb[1, rows] = jnp.dot(lhs[:, :mid_k], rhs[1][:mid_k], preferred_element_type=F32)
-        pb[3, rows] = jnp.dot(lhs[:, mid_k:], rhs[1][mid_k:], preferred_element_type=F32)
+        h = half_rows // 2
+        pb[1, half * half_rows : half * half_rows + h] = jnp.dot(lhs[:h], rhs[1], preferred_element_type=F32)
+        pb[1, half * half_rows + h : (half + 1) * half_rows] = jnp.dot(lhs[h:], rhs[1], preferred_element_type=F32)
 
     def gathered(f, bias):
         rows = slice(f * COLS, (f + 1) * COLS)
         col = lax.broadcasted_iota(jnp.int32, (COLS, 2 * C), 0)
         low = jnp.where(col == 0, 0.0, pltpu.roll(pb[0, rows], 1, 0))
         high = jnp.where(col == COLS - 1, 0.0, pltpu.roll(pb[2, rows], COLS - 1, 0))
-        y = (low + pb[1, rows]) + (pb[3, rows] + high)
+        y = (low + pb[1, rows]) + high
         return y[:, 0:C] + bias, y[:, C : 2 * C] + bias
 
     def gather_mid(frames, total):
@@ -313,7 +389,12 @@
     x = xa[...].astype(F32).reshape(SPAN * ROWS, COLS, C)
     mean = jnp.sum(jnp.sum(x, axis=0), axis=0, keepdims=True) * (1.0 / n_local)
     pl.semaphore_wait(barrier, expected)
-    send_stats(0, mean, xa)
+    first_exchange(mean)
+
+    @pl.when(has_prev)
+    def _():
+        pl.semaphore_signal(go.at[0], inc=1, device_id=dev(-1, 0), device_id_type=MESH)
+
     halo1 = halo(0, acts)
     start_all(halo1)
     caches = [cache_copies(0, cache1), cache_copies(1, cache2)]
@@ -334,50 +415,46 @@
 
     early, late = range(2, SPAN), range(2)
 
-    def stage(conv, src, scale, shift):
-        wait_stats(conv)
-        combine(conv, scale)
-        send_mv = mv_copy(conv)
-
-        @pl.when(has_next)
-        def _():
-            send_mv.start()
-
+    def stage(conv, src, scale, shift, n_jobs):
+        finish(0, pieces_of(True) if conv == 0 else [(full[0], 1)], scale)
         wait_halo(conv, 0, hl.at[conv], has_up)
         wait_halo(conv, 1, hr.at[conv], has_down)
         fill(conv, src, shift, early)
         conv_half((wb1, wb2)[conv], 1)
         fill(conv, src, shift, late)
-        wait_prev(conv)
+        wait_prev(conv, n_jobs)
+        finish(1, pieces_of(False) if conv == 0 else [(full[1], 1)], scale)
         fill_prev(conv, shift)
         conv_half((wb1, wb2)[conv], 0)
-        return send_mv
-
-    send_mv = stage(0, xa, par[0:1], 0.5 * par[1:2])
+
+    n_jobs = second_hop()
+    stage(0, xa, par[0:1], 0.5 * par[1:2], n_jobs)
     total = gather_mid(range(4, SPAN), jnp.zeros((COLS, C), F32))
     total = gather_mid(range(4), total)
 
-    send_stats(1, jnp.sum(total, axis=0, keepdims=True) * (1.0 / n_local), mid)
+    second_exchange(jnp.sum(total, axis=0, keepdims=True) * (1.0 / n_local))
     halo2 = halo(1, mid)
     start_all(halo2)
     wait_send_all(halo1)
     for _, remote in caches:
         wait_send_all(remote, first)
-    wait_stats_sent(0)
+    bulk_wait(win.at[pl.ds(0, n_win - 1)], win_send)
+    bulk_wait(part.at[0, pl.ds(0, n_jobs)], part_send.at[0])
 
     @pl.when(has_next)
     def _():
-        send_mv.wait_send()
-
-    send_mv2 = stage(1, mid, par[3:4], 0.5 * par[4:5])
+        bulk_wait(part.at[0, pl.ds(0, n_jobs + 1)], part_send.at[1])
+
+    bulk_wait(full.at[0, pl.ds(0, n_row - 1)], full_recv.at[0])
+    stage(1, mid, par[3:4], 0.5 * par[4:5], n_jobs)
     gather_out(range(4, SPAN))
     gather_out(range(4))
     wait_send_all(halo2)
-    wait_stats_sent(1)
+    bulk_wait(full.at[0, pl.ds(0, n_row - 1)], full_send.at[0])
 
     @pl.when(has_next)
     def _():
-        send_mv2.wait_send()
+        bulk_wait(full.at[0], full_send.at[1])
 
 
 def solution(mesh):
@@ -397,22 +474,27 @@
                 pltpu.VMEM((3, 3, 4 * C, 2 * C), BF16),
                 pltpu.VMEM((3, 3, 4 * C, 2 * C), BF16),
                 pltpu.VMEM((SPAN + 2, COLS, 4 * C), BF16),
-                pltpu.VMEM((4, SPAN * COLS, 2 * C), F32),
+                pltpu.VMEM((3, SPAN * COLS, 2 * C), F32),
                 pltpu.VMEM((2, SPAN, COLS, C), BF16),
                 pltpu.VMEM((2, SPAN, COLS, C), BF16),
                 pltpu.VMEM((2, 2, 4, COLS, C), BF16),
+                pltpu.VMEM((2 * (2 * (n_row // 8) + 1), 2, C), F32),
+                pltpu.VMEM((3, 3, 2, C), F32),
                 pltpu.VMEM((2, n_row, 2, C), F32),
-                pltpu.VMEM((2, 2, 2, C), F32),
+                pltpu.VMEM((2, 2, C), F32),
                 pltpu.SemaphoreType.DMA((7,)),
                 pltpu.SemaphoreType.DMA((2, 6)),
                 pltpu.SemaphoreType.DMA((2, 5)),
                 pltpu.SemaphoreType.DMA((2, 5)),
                 pltpu.SemaphoreType.DMA((2, 2)),
                 pltpu.SemaphoreType.DMA((2,)),
+                pltpu.SemaphoreType.DMA,
+                pltpu.SemaphoreType.DMA,
                 pltpu.SemaphoreType.DMA((2,)),
                 pltpu.SemaphoreType.DMA((2,)),
                 pltpu.SemaphoreType.DMA((2,)),
                 pltpu.SemaphoreType.DMA((2,)),
+                pltpu.SemaphoreType.REGULAR((2,)),
             ],
             compiler_params=pltpu.CompilerParams(collective_id=0, has_side_effects=True),
         )(*args)

time: 41.2 us -> 37.2 us (0.903); the launches traced: 40.5 us -> 37 us
  Pallas kernels: 38.8 us -> 35.4 us
    pallas_call x1, Pallas kernels: 38.8 us -> 35.4 us  [step(): pl.pallas_call(functools.partial(kernel, n_sec, n_row), out_shape=jax.Sha...]
where the time goes in v3:
time: 37.2 us; the launch traced here: 37 us
  Pallas kernels  35.4 us (95%)
  local copies, waits for them, and re-layouts  1.67 us (4%)
    pallas_call x1, Pallas kernels, step(): pl.pallas_call(functools.partial(kernel, n_sec, n_row), out_shape=jax.Sha...  35.4 us
    unnamed x1, local copies, waits for them, and re-layouts  1.67 us

profile of v3, /device:TPU:25, one launch (start us, length us, event | category | flops | bytes accessed | tf_op | source)
XLA Modules:
  0.0 37.0 jit_solution(16286941350729980955)
XLA Ops:
  0.0 35.4 %shard_map.109 = bf16[8,2,64,128]{3,2,1,0:T(8,128)(2,1)} custom-call(bf16[8,2,64,128]{3,2,1,0:T(8,128)(2,1)} %acts.1, bf16[2,2,64,128]{3,2,1,0:T(8,128)(2,1)} %cache1.1, bf16[2,2,64,128]{3,2,1,0:T(8,128)(2,1)} %cache2.1, f32[128]{0:T(128)} %g1.1, f32[128]{0:T(128)} %b1.1, bf16[3,3,3,128,128]{4,3,2,1,0:T(8,128)(2,1)} %w1.1, f32[128]{0:T(128)} %bias1.1, ...), custom_call_target="tpu_custom_call" | custom-call | tf_op jit(solution)/shard_map/pallas_call | solution.py:465
  35.4 1.7 %copy.13 = bf16[8,2,64,128]{3,2,1,0:T(8,128)(2,1)} copy(bf16[8,2,64,128]{3,2,1,0:T(8,128)(2,1)} %shard_map.109) | data formatting | bytes 524288

commit v4 on v3

--- a/solution.py
+++ b/solution.py
@@ -348,21 +348,15 @@
                     y = jnp.where(cond, y, 0.0)
                 u[f, :, slot * C : (slot + 1) * C] = y.astype(BF16)
 
-    half_rows = SPAN // 2 * COLS
-    mid_k = 6 * C
-
-    def conv_half(wb, half):
-        f0 = half * (SPAN // 2)
-        rows = slice(half * half_rows, (half + 1) * half_rows)
-        lhs = jnp.concatenate(
-            [u[f0 + dt : f0 + dt + SPAN // 2].reshape(half_rows, 4 * C) for dt in range(3)], axis=1
-        )
+    def conv_frames(wb, f0, f1):
+        count, mid_row = (f1 - f0) * COLS, (f0 + f1) // 2 * COLS
+        lhs = jnp.concatenate([u[f0 + dt : f1 + dt].reshape(count, 4 * C) for dt in range(3)], axis=1)
         rhs = [jnp.concatenate([wb[dt, dw] for dt in range(3)], axis=0) for dw in range(3)]
-        pb[0, rows] = jnp.dot(lhs, rhs[0], preferred_element_type=F32)
-        pb[2, rows] = jnp.dot(lhs, rhs[2], preferred_element_type=F32)
-        h = half_rows // 2
-        pb[1, half * half_rows : half * half_rows + h] = jnp.dot(lhs[:h], rhs[1], preferred_element_type=F32)
-        pb[1, half * half_rows + h : (half + 1) * half_rows] = jnp.dot(lhs[h:], rhs[1], preferred_element_type=F32)
+        lo, hi = f0 * COLS, f1 * COLS
+        for dw in (0, 2):
+            pb[dw, lo:hi] = jnp.dot(lhs, rhs[dw], preferred_element_type=F32)
+        pb[1, lo:mid_row] = jnp.dot(lhs[: mid_row - lo], rhs[1], preferred_element_type=F32)
+        pb[1, mid_row:hi] = jnp.dot(lhs[mid_row - lo :], rhs[1], preferred_element_type=F32)
 
     def gathered(f, bias):
         rows = slice(f * COLS, (f + 1) * COLS)
@@ -380,7 +374,7 @@
                 total = total + y.astype(F32)
         return total
 
-    def gather_out(frames):
+    def gather_out(frames, carry):
         for f in frames:
             for row, y in enumerate(gathered(f, par[5:6])):
                 out[f, row] = (xa[f, row].astype(F32) + y).astype(BF16)
@@ -413,24 +407,25 @@
     for conv, copy in w_loads:
         copy.wait()
 
-    early, late = range(2, SPAN), range(2)
-
-    def stage(conv, src, scale, shift, n_jobs):
+    cut = 4
+
+    def stage(conv, src, scale, shift, n_jobs, gather, carry):
+        wb = (wb1, wb2)[conv]
         finish(0, pieces_of(True) if conv == 0 else [(full[0], 1)], scale)
         wait_halo(conv, 0, hl.at[conv], has_up)
         wait_halo(conv, 1, hr.at[conv], has_down)
-        fill(conv, src, shift, early)
-        conv_half((wb1, wb2)[conv], 1)
-        fill(conv, src, shift, late)
+        fill(conv, src, shift, range(cut - 2, SPAN))
+        conv_frames(wb, cut, SPAN)
+        fill(conv, src, shift, range(cut - 2))
+        carry = gather(range(cut, SPAN), carry)
         wait_prev(conv, n_jobs)
         finish(1, pieces_of(False) if conv == 0 else [(full[1], 1)], scale)
         fill_prev(conv, shift)
-        conv_half((wb1, wb2)[conv], 0)
+        conv_frames(wb, 0, cut)
+        return gather(range(cut), carry)
 
     n_jobs = second_hop()
-    stage(0, xa, par[0:1], 0.5 * par[1:2], n_jobs)
-    total = gather_mid(range(4, SPAN), jnp.zeros((COLS, C), F32))
-    total = gather_mid(range(4), total)
+    total = stage(0, xa, par[0:1], 0.5 * par[1:2], n_jobs, gather_mid, jnp.zeros((COLS, C), F32))
 
     second_exchange(jnp.sum(total, axis=0, keepdims=True) * (1.0 / n_local))
     halo2 = halo(1, mid)
@@ -446,9 +441,7 @@
         bulk_wait(part.at[0, pl.ds(0, n_jobs + 1)], part_send.at[1])
 
     bulk_wait(full.at[0, pl.ds(0, n_row - 1)], full_recv.at[0])
-    stage(1, mid, par[3:4], 0.5 * par[4:5], n_jobs)
-    gather_out(range(4, SPAN))
-    gather_out(range(4))
+    stage(1, mid, par[3:4], 0.5 * par[4:5], n_jobs, gather_out, None)
     wait_send_all(halo2)
     bulk_wait(full.at[0, pl.ds(0, n_row - 1)], full_send.at[0])
 
@@ -464,7 +457,7 @@
         any_spec = pl.BlockSpec(memory_space=pl.ANY)
         return pl.pallas_call(
             functools.partial(kernel, n_sec, n_row),
-            out_shape=jax.ShapeDtypeStruct((SPAN, ROWS, COLS, C), BF16),
+            out_shape=pltpu.VMEM((SPAN, ROWS, COLS, C), BF16),
             in_specs=[any_spec] * 11,
             out_specs=pl.BlockSpec(memory_space=pltpu.VMEM),
             scratch_shapes=[

time: 37.2 us -> 35.4 us (0.952)
  local copies, waits for them, and re-layouts: 1.67 us -> 0.71 us
  Pallas kernels: 35.4 us -> 34.6 us
    unnamed x1, local copies, waits for them, and re-layouts: 1.67 us -> 0.71 us
    pallas_call x1, Pallas kernels: 35.4 us -> 34.6 us  [step(): pl.pallas_call(functools.partial(kernel, n_sec, n_row), out_shape=pltpu.V...]
where the time goes in v4:
time: 35.4 us; the launch traced here: 35.3 us
  Pallas kernels  34.6 us (98%)
  local copies, waits for them, and re-layouts  0.71 us (2%)
    pallas_call x1, Pallas kernels, step(): pl.pallas_call(functools.partial(kernel, n_sec, n_row), out_shape=pltpu.V...  34.6 us

profile of v4, /device:TPU:25, one launch (start us, length us, event | category | flops | bytes accessed | tf_op | source)
XLA Modules:
  0.0 35.3 jit_solution(11464754007447981643)
XLA Ops:
  0.0 34.6 %shard_map.109 = bf16[8,2,64,128]{3,2,1,0:T(8,128)(2,1)S(1)} custom-call(bf16[8,2,64,128]{3,2,1,0:T(8,128)(2,1)} %acts.1, bf16[2,2,64,128]{3,2,1,0:T(8,128)(2,1)} %cache1.1, bf16[2,2,64,128]{3,2,1,0:T(8,128)(2,1)} %cache2.1, f32[128]{0:T(128)} %g1.1, f32[128]{0:T(128)} %b1.1, bf16[3,3,3,128,128]{4,3,2,1,0:T(8,128)(2,1)} %w1.1, f32[128]{0:T(128)} %bias1.1, ...), custom_call_target="tpu_custom_call" | custom-call | tf_op jit(solution)/shard_map/pallas_call | solution.py:458
  34.6 0.7 %copy.13 = bf16[8,2,64,128]{3,2,1,0:T(8,128)(2,1)} copy(bf16[8,2,64,128]{3,2,1,0:T(8,128)(2,1)S(1)} %shard_map.109) | data formatting | bytes 524288

commit v5 on v4

--- a/solution.py
+++ b/solution.py
@@ -209,8 +209,12 @@
         pltpu.make_async_copy(ref, ref, sem).wait()
 
     def local_stats(mean, src):
-        d = src[...].astype(F32).reshape(SPAN * ROWS, COLS, C) - mean[None]
-        m2 = jnp.sum(jnp.sum(d * d, axis=0), axis=0, keepdims=True)
+        totals = [jnp.zeros((COLS, C), F32), jnp.zeros((COLS, C), F32)]
+        for f in range(SPAN):
+            for row in range(ROWS):
+                d = src[f, row].astype(F32) - mean
+                totals[row] = totals[row] + d * d
+        m2 = jnp.sum(totals[0] + totals[1], axis=0, keepdims=True)
         return jnp.concatenate([mean, m2], axis=0)
 
     def merged(parts, count, size):
@@ -229,9 +233,9 @@
         spread = lane_group_sum(jnp.broadcast_to(q, (8, C)))[0:1] * (1.0 / (4 * n_local * n_row))
         mv[slot] = jnp.concatenate([mean, 0.5 * scale / jnp.sqrt(spread + EPS)], axis=0)
 
-    def first_exchange(mean):
-        mine = 2 * reach + core
-        win[mine] = local_stats(mean, xa)
+    mine = 2 * reach + core
+
+    def first_exchange():
         window(
             lambda offset, peer: send(
                 win.at[mine], win.at[2 * (reach - offset) + core], win_send, win_recv, 0, peer
@@ -240,7 +244,6 @@
 
     def second_hop():
         bulk_wait(win.at[pl.ds(0, n_win - 1)], win_recv)
-        part[0, 0] = merged(win[...], n_win, n_local)
         part[0, 1] = merged(win[n_win - n_fwd :], n_fwd, n_local)
         if n_bwd:
             part[0, 2] = merged(win[2 : 2 + n_bwd], n_bwd, n_local)
@@ -249,6 +252,7 @@
             jobs.append((2, at_chip(reach, core)))
         for i, peer in jobs:
             send(part.at[0, i], part.at[1, i], part_send.at[0], part_recv.at[0], 0, peer)
+        part[0, 0] = merged(win[...], n_win, n_local)
 
         @pl.when(has_next)
         def _():
@@ -282,11 +286,11 @@
         def one(offset):
             peer = r + offset
             peer = jnp.where(peer >= n_row, peer - n_row, peer)
-            send(full.at[0, r], full.at[0, r], full_send.at[0], full_recv.at[0], 0, peer)
-
             @pl.when(has_next)
             def _():
                 send(full.at[0, r], full.at[1, r], full_send.at[1], full_recv.at[1], 1, peer)
+
+            send(full.at[0, r], full.at[0, r], full_send.at[0], full_recv.at[0], 0, peer)
 
         half = n_row // 2
         one(half)
@@ -349,21 +353,46 @@
                 u[f, :, slot * C : (slot + 1) * C] = y.astype(BF16)
 
     def conv_frames(wb, f0, f1):
-        count, mid_row = (f1 - f0) * COLS, (f0 + f1) // 2 * COLS
-        lhs = jnp.concatenate([u[f0 + dt : f1 + dt].reshape(count, 4 * C) for dt in range(3)], axis=1)
-        rhs = [jnp.concatenate([wb[dt, dw] for dt in range(3)], axis=0) for dw in range(3)]
         lo, hi = f0 * COLS, f1 * COLS
-        for dw in (0, 2):
-            pb[dw, lo:hi] = jnp.dot(lhs, rhs[dw], preferred_element_type=F32)
-        pb[1, lo:mid_row] = jnp.dot(lhs[: mid_row - lo], rhs[1], preferred_element_type=F32)
-        pb[1, mid_row:hi] = jnp.dot(lhs[mid_row - lo :], rhs[1], preferred_element_type=F32)
+        shape = (hi - lo, 2 * C)
+        pl.run_scoped(
+            functools.partial(conv_scoped, wb, f0, f1),
+            pltpu.ACC(0)(shape, F32),
+            pltpu.ACC(0)(shape, F32),
+            pltpu.ACC(1)(shape, F32),
+            pltpu.ACC(1)(shape, F32),
+        )
+
+    def conv_scoped(wb, f0, f1, acc0, acc1, acc2, acc3):
+        lo, hi = f0 * COLS, f1 * COLS
+        deep = 2 * C
+
+        def lhs_tile(k):
+            dt, lane = k // 2, k % 2 * deep
+            return u[f0 + dt : f1 + dt, :, lane : lane + deep].reshape(hi - lo, deep)
+
+        def rhs_tile(dw, k):
+            dt, row = k // 2, k % 2 * deep
+            return wb[dt, dw, row : row + deep, :]
+
+        plans = (
+            [(acc0, 0, k) for k in range(6)] + [(acc1, 1, k) for k in range(3)],
+            [(acc2, 2, k) for k in range(6)] + [(acc3, 1, k) for k in range(3, 6)],
+        )
+        for i in range(9):
+            for mxu, plan in enumerate(plans):
+                acc, dw, k = plan[i]
+                pltpu.matmul_push_rhs(rhs_tile(dw, k), i % 2, mxu)
+                pltpu.matmul_acc_lhs(acc, lhs_tile(k), load_staged_rhs=i % 2)
+        for slot, acc in ((0, acc0), (2, acc2), (1, acc1), (3, acc3)):
+            pb[slot, lo:hi] = pltpu.matmul_pop(acc)
 
     def gathered(f, bias):
         rows = slice(f * COLS, (f + 1) * COLS)
         col = lax.broadcasted_iota(jnp.int32, (COLS, 2 * C), 0)
         low = jnp.where(col == 0, 0.0, pltpu.roll(pb[0, rows], 1, 0))
         high = jnp.where(col == COLS - 1, 0.0, pltpu.roll(pb[2, rows], COLS - 1, 0))
-        y = (low + pb[1, rows]) + high
+        y = (low + pb[1, rows]) + (pb[3, rows] + high)
         return y[:, 0:C] + bias, y[:, C : 2 * C] + bias
 
     def gather_mid(frames, total):
@@ -382,8 +411,9 @@
     load_x.wait()
     x = xa[...].astype(F32).reshape(SPAN * ROWS, COLS, C)
     mean = jnp.sum(jnp.sum(x, axis=0), axis=0, keepdims=True) * (1.0 / n_local)
+    win[mine] = local_stats(mean, xa)
     pl.semaphore_wait(barrier, expected)
-    first_exchange(mean)
+    first_exchange()
 
     @pl.when(has_prev)
     def _():
@@ -467,7 +497,7 @@
                 pltpu.VMEM((3, 3, 4 * C, 2 * C), BF16),
                 pltpu.VMEM((3, 3, 4 * C, 2 * C), BF16),
                 pltpu.VMEM((SPAN + 2, COLS, 4 * C), BF16),
-                pltpu.VMEM((3, SPAN * COLS, 2 * C), F32),
+                pltpu.VMEM((4, SPAN * COLS, 2 * C), F32),
                 pltpu.VMEM((2, SPAN, COLS, C), BF16),
                 pltpu.VMEM((2, SPAN, COLS, C), BF16),
                 pltpu.VMEM((2, 2, 4, COLS, C), BF16),

time: 35.4 us -> 35.3 us (level)
  no operation moved by 1% of the time
where the time goes in v5:
time: 35.3 us; the launch traced here: 35.2 us
  Pallas kernels  34.5 us (98%)
  local copies, waits for them, and re-layouts  0.71 us (2%)
    pallas_call x1, Pallas kernels, step(): pl.pallas_call(functools.partial(kernel, n_sec, n_row), out_shape=pltpu.V...  34.5 us

profile of v5, /device:TPU:25, one launch (start us, length us, event | category | flops | bytes accessed | tf_op | source)
XLA Modules:
  0.0 35.2 jit_solution(3038810294210278748)
XLA Ops:
  0.0 34.5 %shard_map.109 = bf16[8,2,64,128]{3,2,1,0:T(8,128)(2,1)S(1)} custom-call(bf16[8,2,64,128]{3,2,1,0:T(8,128)(2,1)} %acts.1, bf16[2,2,64,128]{3,2,1,0:T(8,128)(2,1)} %cache1.1, bf16[2,2,64,128]{3,2,1,0:T(8,128)(2,1)} %cache2.1, f32[128]{0:T(128)} %g1.1, f32[128]{0:T(128)} %b1.1, bf16[3,3,3,128,128]{4,3,2,1,0:T(8,128)(2,1)} %w1.1, f32[128]{0:T(128)} %bias1.1, ...), custom_call_target="tpu_custom_call" | custom-call | tf_op jit(solution)/shard_map/pallas_call | solution.py:488
  34.5 0.7 %copy.13 = bf16[8,2,64,128]{3,2,1,0:T(8,128)(2,1)} copy(bf16[8,2,64,128]{3,2,1,0:T(8,128)(2,1)S(1)} %shard_map.109) | data formatting | bytes 524288
